TPU v7x, 32 devices: a whole 2x2x4 slice. The times are simulated.
32 devices in a mesh: band: 4 (over x, core), grid: 8 (over z, y).
Axes of the slice: x: 2, y: 2, z: 4, core: 2. Of those that a mesh axis runs over, the one named last changes fastest.
Arguments:
- orbitals: float32 [4, 128, 128, 128], P('band', 'grid'), may hold values from -4 to 10, as said below
- pivots: int32 [4], replicated, may hold values from 0 to 2097151, as said below
- pattern: int32 [4, 4], replicated, may hold values from 0 to 1, as said below
Outputs:
- localized: float32 [4, 128, 128, 128], P('band', 'grid')
- exchange_term: float32 [4, 128, 128, 128], P('band', 'grid')
Inputs may be any that keep to these rules, and one draw needn't show every extreme that they name: Values of the orbitals on the grid; the matrix of their values at the pivots has a Cholesky factorization. `pivots`: distinct flat cell indices; the first and the last cell of the grid are always among them. `pattern`: every diagonal entry is 1; each row holds 1 to 4 ones, some row exactly 4; the matrix holds exactly 8 ones.
All inputs are finite; a program needn't handle non-finite values.
Results may differ from a plain program's by a relative error of at most 0.0003.
Values sent between devices are 32-bit elements; how exact they have to be, the bound alone decides.
A program may use at most 64 MiB of HBM per device.

v0:
```python
import jax
import jax.numpy as jnp
from jax import lax
from jax.sharding import PartitionSpec as P

MOST_PARTNERS = 4
precise = lax.Precision.HIGHEST


def tables(length):
    across = jnp.arange(length, dtype=jnp.int32)
    phases = across[:, None] * across[None, :] % length
    angles = phases.astype(jnp.float32) * (2.0 * jnp.pi / length)
    return (jnp.cos(angles), jnp.sin(angles))


def wrapped(indices, length):
    return jnp.where(indices < length // 2, indices, indices - length)


def coulomb(length, plane_start, plane_count):
    wave_first = wrapped(jnp.arange(length, dtype=jnp.int32), length).astype(jnp.float32)
    wave_second = wrapped(plane_start + jnp.arange(plane_count, dtype=jnp.int32), length).astype(
        jnp.float32
    )
    squared = (
        wave_first[:, None, None] ** 2
        + wave_second[None, :, None] ** 2
        + wave_first[None, None, :] ** 2
    )
    scaling = float(length) ** 1.5
    return jnp.where(squared > 0, 0.25 / (scaling * jnp.maximum(squared, 1.0)), 0.0)


def densities(first_bands, second_bands):
    return (first_bands[:, None] * second_bands[None, :]).reshape((-1,) + first_bands.shape[1:])


def applied(potential, first_bands, second_bands):
    shaped = potential.reshape(
        (first_bands.shape[0], second_bands.shape[0]) + first_bands.shape[1:]
    )
    return jnp.sum(shaped * second_bands[None], axis=1)


def filtered(real_in, imag_in, kernel, cos_table, sin_table):
    real_part = jnp.dot(real_in, cos_table, precision=precise) + jnp.dot(
        imag_in, sin_table, precision=precise
    )
    imag_part = jnp.dot(imag_in, cos_table, precision=precise) - jnp.dot(
        real_in, sin_table, precision=precise
    )
    real_part, imag_part = (
        jnp.einsum("pxyz,yk->pxkz", real_part, cos_table, precision=precise)
        + jnp.einsum("pxyz,yk->pxkz", imag_part, sin_table, precision=precise),
        jnp.einsum("pxyz,yk->pxkz", imag_part, cos_table, precision=precise)
        - jnp.einsum("pxyz,yk->pxkz", real_part, sin_table, precision=precise),
    )
    real_wide = lax.all_to_all(real_part, "grid", split_axis=2, concat_axis=1, tiled=True)
    imag_wide = lax.all_to_all(imag_part, "grid", split_axis=2, concat_axis=1, tiled=True)
    ahead_real = (
        jnp.einsum("pxyz,xk->pkyz", real_wide, cos_table, precision=precise)
        + jnp.einsum("pxyz,xk->pkyz", imag_wide, sin_table, precision=precise)
    ) * kernel
    ahead_imag = (
        jnp.einsum("pxyz,xk->pkyz", imag_wide, cos_table, precision=precise)
        - jnp.einsum("pxyz,xk->pkyz", real_wide, sin_table, precision=precise)
    ) * kernel
    back_real = jnp.einsum("pxyz,xk->pkyz", ahead_real, cos_table, precision=precise) - jnp.einsum(
        "pxyz,xk->pkyz", ahead_imag, sin_table, precision=precise
    )
    back_imag = jnp.einsum("pxyz,xk->pkyz", ahead_imag, cos_table, precision=precise) + jnp.einsum(
        "pxyz,xk->pkyz", ahead_real, sin_table, precision=precise
    )
    real_part = lax.all_to_all(back_real, "grid", split_axis=1, concat_axis=2, tiled=True)
    imag_part = lax.all_to_all(back_imag, "grid", split_axis=1, concat_axis=2, tiled=True)
    real_part, imag_part = (
        jnp.einsum("pxyz,yk->pxkz", real_part, cos_table, precision=precise)
        - jnp.einsum("pxyz,yk->pxkz", imag_part, sin_table, precision=precise),
        jnp.einsum("pxyz,yk->pxkz", imag_part, cos_table, precision=precise)
        + jnp.einsum("pxyz,yk->pxkz", real_part, sin_table, precision=precise),
    )
    out_real = jnp.dot(real_part, cos_table, precision=precise) - jnp.dot(
        imag_part, sin_table, precision=precise
    )
    out_imag = jnp.dot(imag_part, cos_table, precision=precise) + jnp.dot(
        real_part, sin_table, precision=precise
    )
    return (out_real, out_imag)


def twin_potential(first_one, second_one, first_two, second_two, kernel, cos_table, sin_table):
    potential_one, potential_two = filtered(
        densities(first_one, second_one),
        densities(first_two, second_two),
        kernel,
        cos_table,
        sin_table,
    )
    return (
        applied(potential_one, first_one, second_one),
        applied(potential_two, first_two, second_two),
    )


def collect(wanted, portion):
    positions = jnp.arange(portion.shape[0], dtype=jnp.int32)
    chooser = (wanted[:, None] == positions[None, :]).astype(jnp.float32)
    return jnp.einsum("qm,mxyz->qxyz", chooser, portion, precision=precise)


def local(orbitals, pivots, pattern):
    band_dev = orbitals.shape[0]
    slab_planes = orbitals.shape[1]
    length = orbitals.shape[3]
    block_total = pattern.shape[0]
    grid_index = lax.axis_index("grid")
    band_index = lax.axis_index("band")
    cell_count = slab_planes * length * length
    flat_local = orbitals.reshape(band_dev, cell_count)
    local_cell = pivots - grid_index * cell_count
    inside = (local_cell >= 0) & (local_cell < cell_count)
    sampled = jnp.take(flat_local, jnp.clip(local_cell, 0, cell_count - 1), axis=1)
    partial_pick = jnp.where(inside[None, :], sampled, 0.0)
    own_rows = lax.psum(partial_pick, "grid")
    picked = lax.all_gather(own_rows, "band", axis=0, tiled=True)
    gram_matrix = jnp.dot(picked.T, picked, precision=precise)
    factor = jnp.linalg.cholesky(gram_matrix)
    rotation = lax.linalg.triangular_solve(factor, picked.T, left_side=True, lower=True).T
    own_weights = lax.dynamic_slice_in_dim(rotation, band_index * band_dev, band_dev, 0)
    localized = lax.psum_scatter(
        jnp.einsum("bk,bxyz->kxyz", own_weights, orbitals, precision=precise),
        "band",
        scatter_dimension=0,
        tiled=True,
    )
    cos_table, sin_table = tables(length)
    plane_count = length // lax.axis_size("grid")
    kernel = coulomb(length, grid_index * plane_count, plane_count)
    columns = jnp.arange(block_total, dtype=jnp.int32)
    members = jnp.arange(band_dev, dtype=jnp.int32)
    own_row = lax.dynamic_index_in_dim(pattern, band_index, 0, keepdims=False)
    before = jnp.cumsum(own_row) - own_row
    slot_ids = jnp.arange(MOST_PARTNERS, dtype=jnp.int32)
    matches = (own_row[None, :] == 1) & (before[None, :] == slot_ids[:, None])
    partner = jnp.sum(jnp.where(matches, columns[None, :], 0), axis=1)
    present = jnp.any(matches, axis=1)
    wanted = jnp.where(
        present[:, None], partner[:, None] * band_dev + members[None, :], -1
    ).reshape(-1)
    partners = collect(wanted, lax.all_gather(localized, "band", axis=0, tiled=True))
    exchange_term = jnp.zeros_like(localized)
    for couple in range(MOST_PARTNERS // 2):
        first_rows = partners[2 * couple * band_dev : (2 * couple + 1) * band_dev]
        second_rows = partners[(2 * couple + 1) * band_dev : (2 * couple + 2) * band_dev]
        term_one, term_two = twin_potential(
            localized, first_rows, localized, second_rows, kernel, cos_table, sin_table
        )
        exchange_term = exchange_term + term_one + term_two
    return (localized, exchange_term)


def solution(mesh):
    return jax.shard_map(
        local,
        mesh=mesh,
        in_specs=(P("band", "grid", None, None), P(), P()),
        out_specs=(P("band", "grid", None, None), P("band", "grid", None, None)),
        check_vma=False,
    )
```

profile of v0, /device:TPU:0, one launch (start us, length us, event | category | flops | bytes accessed | tf_op | source)
XLA Modules:
  0.0 410.0 jit_solution(14240325148722384985)
XLA Ops:
  10.0 23.1 %psum.7 = f32[1,4]{1,0:T(1,128)S(1)} all-reduce(f32[1,4]{1,0:T(1,128)S(1)} %fusion.210), channel_id=1, replica_groups=mesh['band'=4,'grid'=8] {'grid'}, use_global_device_ids=true, to_apply=%region_0.1 | all-reduce | flops 4 | bytes 32 | tf_op jit(solution)/shard_map/psum | solution.py:125
  33.1 5.0 %all-gather = f32[4,1,4]{2,1,0:T(1,128)S(1)} all-gather(f32[1,1,4]{2,1,0:T(1,128)S(1)} %bitcast.338), channel_id=1, replica_groups=mesh['band'=4,'grid'=8] {'band'}, dimensions={0}, use_global_device_ids=true | all-gather | bytes 80 | tf_op jit(solution)/shard_map/all_gather | solution.py:126
  40.6 3.8 broadcast_multiply_fusion
  44.4 41.9 %reduce-scatter.2.cloned.1.call-done = f32[1,16,128,128]{3,2,1,0:T(8,128)} async-done(((f32[4,16,128,128]{3,2,1,0:T(8,128)}), f32[1,16,128,128]{3,2,1,0:T(8,128)}) %reduce-scatter.2.cloned.1.call-update) | async-done | bytes 1048592 | tf_op jit(solution)/shard_map/reduce_scatter | solution.py:131
  87.5 35.6 %all-gather.3.cloned.1.call-done = f32[4,16,128,128]{3,2,1,0:T(8,128)} async-done(((f32[1,16,128,128]{3,2,1,0:T(8,128)}), f32[4,16,128,128]{3,2,1,0:T(8,128)}) %all-gather.3.cloned.1.call-update) | async-done | bytes 4194320 | tf_op jit(solution)/shard_map/all_gather | solution.py:151
  123.0 8.5 %fusion = f32[4,16,128,128]{3,0,2,1:T(4,128)S(1)} fusion(f32[4,16,128,128]{3,2,1,0:T(8,128)} %all-gather.3.cloned.1.call-done, s32[4]{0:T(128)S(1)} %broadcast_select_fusion), kind=kOutput, calls=%fused_computation.1 | convolution fusion | flops 50331664 | bytes 8388624 | tf_op jit(solution)/shard_map/qm,mxyz->qxyz/dot_general | solution.py:109
  131.6 3.6 slice_multiply_fusion.3
  145.2 5.8 %all-to-all-start.4 = ((f32[1,16,128,128]{3,1,0,2:T(8,128)}), f32[1,16,128,128]{3,1,0,2:T(8,128)}, u32[]{:S(2)}, u32[]{:S(2)}) async-start(f32[1,16,128,128]{3,1,0,2:T(8,128)} %copy.182), calls=%async_computation.5 | async-start | bytes 2097152 | tf_op jit(solution)/shard_map/all_to_all | solution.py:59
  152.3 2.5 fusion.8
  154.8 1.6 copy.187
  156.4 20.8 %all-to-all-done.4 = f32[1,16,128,128]{3,1,0,2:T(8,128)} async-done(((f32[1,16,128,128]{3,1,0,2:T(8,128)}), f32[1,16,128,128]{3,1,0,2:T(8,128)}, u32[]{:S(2)}, u32[]{:S(2)}) %all-to-all-start.4) | async-done | bytes 1048608 | tf_op jit(solution)/shard_map/all_to_all | solution.py:59
  177.2 4.2 %all-to-all-start.5 = ((f32[1,16,128,128]{3,1,0,2:T(8,128)}), f32[1,16,128,128]{3,1,0,2:T(8,128)}, u32[]{:S(2)}, u32[]{:S(2)}) async-start(f32[1,16,128,128]{3,1,0,2:T(8,128)} %copy.187), calls=%async_computation.6 | async-start | bytes 2097152 | tf_op jit(solution)/shard_map/all_to_all | solution.py:60
  190.5 16.5 %all-to-all-done.5 = f32[1,16,128,128]{3,1,0,2:T(8,128)} async-done(((f32[1,16,128,128]{3,1,0,2:T(8,128)}), f32[1,16,128,128]{3,1,0,2:T(8,128)}, u32[]{:S(2)}, u32[]{:S(2)}) %all-to-all-start.5) | async-done | bytes 1048608 | tf_op jit(solution)/shard_map/all_to_all | solution.py:60
  207.1 4.0 all-to-all-start.1
  213.7 1.6 copy.156
  215.3 21.6 %all-to-all-done.1 = f32[1,16,128,128]{3,1,0,2:T(8,128)S(1)} async-done(((f32[1,16,128,128]{3,1,0,2:T(8,128)}), f32[1,16,128,128]{3,1,0,2:T(8,128)S(1)}, u32[]{:S(2)}, u32[]{:S(2)}) %all-to-all-start.1) | async-done | bytes 1048608 | tf_op jit(solution)/shard_map/all_to_all | solution.py:60
  236.8 3.6 all-to-all-start
  251.4 1.6 copy.194
  253.0 13.5 %all-to-all-done = f32[1,16,128,128]{3,1,0,2:T(8,128)S(1)} async-done(((f32[1,16,128,128]{3,1,0,2:T(8,128)}), f32[1,16,128,128]{3,1,0,2:T(8,128)S(1)}, u32[]{:S(2)}, u32[]{:S(2)}) %all-to-all-start) | async-done | bytes 1048608 | tf_op jit(solution)/shard_map/all_to_all | solution.py:59
  267.4 3.8 all-to-all-start.6
  273.8 1.6 copy.199
  275.4 21.8 %all-to-all-done.6 = f32[1,128,16,128]{3,2,0,1:T(8,128)S(1)} async-done(((f32[1,128,16,128]{3,2,0,1:T(8,128)}), f32[1,128,16,128]{3,2,0,1:T(8,128)S(1)}, u32[]{:S(2)}, u32[]{:S(2)}) %all-to-all-start.6) | async-done | bytes 1048608 | tf_op jit(solution)/shard_map/all_to_all | solution.py:75
  297.2 4.2 %all-to-all-start.7 = ((f32[1,128,16,128]{3,2,0,1:T(8,128)}), f32[1,128,16,128]{3,2,0,1:T(8,128)}, u32[]{:S(2)}, u32[]{:S(2)}) async-start(f32[1,128,16,128]{3,2,0,1:T(8,128)} %copy.199), calls=%async_computation.8 | async-start | bytes 2097152 | tf_op jit(solution)/shard_map/all_to_all | solution.py:76
  309.8 1.6 copy.173
  311.4 15.6 %all-to-all-done.7 = f32[1,128,16,128]{3,2,0,1:T(8,128)} async-done(((f32[1,128,16,128]{3,2,0,1:T(8,128)}), f32[1,128,16,128]{3,2,0,1:T(8,128)}, u32[]{:S(2)}, u32[]{:S(2)}) %all-to-all-start.7) | async-done | bytes 1048608 | tf_op jit(solution)/shard_map/all_to_all | solution.py:76
  327.1 4.6 %all-to-all-start.3 = ((f32[1,128,16,128]{3,2,0,1:T(8,128)}), f32[1,128,16,128]{3,2,0,1:T(8,128)}, u32[]{:S(2)}, u32[]{:S(2)}) async-start(f32[1,128,16,128]{3,2,0,1:T(8,128)} %copy.173), calls=%async_computation.4 | async-start | bytes 2097152 | tf_op jit(solution)/shard_map/all_to_all | solution.py:76
  334.3 1.6 copy.168
  337.3 2.3 fusion.48
  339.6 17.5 %all-to-all-done.3 = f32[1,128,16,128]{3,2,0,1:T(8,128)} async-done(((f32[1,128,16,128]{3,2,0,1:T(8,128)}), f32[1,128,16,128]{3,2,0,1:T(8,128)}, u32[]{:S(2)}, u32[]{:S(2)}) %all-to-all-start.3) | async-done | bytes 1048608 | tf_op jit(solution)/shard_map/all_to_all | solution.py:76
  357.1 4.2 %all-to-all-start.2 = ((f32[1,128,16,128]{3,2,0,1:T(8,128)}), f32[1,128,16,128]{3,2,0,1:T(8,128)}, u32[]{:S(2)}, u32[]{:S(2)}) async-start(f32[1,128,16,128]{3,2,0,1:T(8,128)} %copy.168), calls=%async_computation.3 | async-start | bytes 2097152 | tf_op jit(solution)/shard_map/all_to_all | solution.py:75
  371.6 15.2 %all-to-all-done.2 = f32[1,128,16,128]{3,2,0,1:T(8,128)} async-done(((f32[1,128,16,128]{3,2,0,1:T(8,128)}), f32[1,128,16,128]{3,2,0,1:T(8,128)}, u32[]{:S(2)}, u32[]{:S(2)}) %all-to-all-start.2) | async-done | bytes 1048608 | tf_op jit(solution)/shard_map/all_to_all | solution.py:75
  398.4 4.5 %multiply_add_fusion = f32[1,16,128,128]{3,0,2,1:T(1,128)} fusion(f32[1,16,128,128]{3,0,2,1:T(1,128)S(1)} %bitcast.318, f32[1,16,128,128]{3,0,2,1:T(1,128)S(1)} %bitcast.317, f32[1,16,128,128]{3,0,2,1:T(1,128)S(1)} %bitcast.319, f32[1,16,128,128]{3,0,2,1:T(1,128)S(1)} %bitcast.320, f32[4,16,128,128]{3,0,2,1:T(4,128)S(1)} %copy-done.1), kind=kLoop, calls=%fused_computation.49 | loop fusion | flops 1835008 | bytes 9437184 | tf_op jit(solution)/shard_map/add | solution.py:159
  (101 shorter events, 77.8 us)
Async XLA Ops:
  7.2 79.1 %reduce-scatter.2.cloned.1.call-start = ((), (), s32[]{:S(2)}) async-start(), calls=%async_computation.9 | async-start | bytes 5242880 | tf_op jit(solution)/shard_map/reduce_scatter | solution.py:131
  44.4 78.6 %all-gather.3.cloned.1.call-start = ((), (), s32[]{:S(2)}) async-start(), calls=%async_computation.10 | async-start | bytes 5242880 | tf_op jit(solution)/shard_map/all_gather | solution.py:151
  87.5 44.1 %copy-start.3 = (f32[1,16,128,128]{3,2,1,0:T(8,128)S(1)}, f32[1,16,128,128]{3,2,1,0:T(8,128)}, u32[]{:S(2)}) copy-start(f32[1,16,128,128]{3,2,1,0:T(8,128)} %reduce-scatter.2.cloned.1.call-done) | copy-start | bytes 3145732
  131.6 3.6 copy-start
  140.1 1.0 copy-start.2
  145.2 32.0 %all-to-all-start.4 = ((f32[1,16,128,128]{3,1,0,2:T(8,128)}), f32[1,16,128,128]{3,1,0,2:T(8,128)}, u32[]{:S(2)}, u32[]{:S(2)}) async-start(f32[1,16,128,128]{3,1,0,2:T(8,128)} %copy.182), calls=%async_computation.5 | async-start | bytes 2097152 | tf_op jit(solution)/shard_map/all_to_all | solution.py:59
  177.2 29.9 %all-to-all-start.5 = ((f32[1,16,128,128]{3,1,0,2:T(8,128)}), f32[1,16,128,128]{3,1,0,2:T(8,128)}, u32[]{:S(2)}, u32[]{:S(2)}) async-start(f32[1,16,128,128]{3,1,0,2:T(8,128)} %copy.187), calls=%async_computation.6 | async-start | bytes 2097152 | tf_op jit(solution)/shard_map/all_to_all | solution.py:60
  207.1 29.7 %all-to-all-start.1 = ((f32[1,16,128,128]{3,1,0,2:T(8,128)}), f32[1,16,128,128]{3,1,0,2:T(8,128)S(1)}, u32[]{:S(2)}, u32[]{:S(2)}) async-start(f32[1,16,128,128]{3,1,0,2:T(8,128)} %copy.161), calls=%async_computation.2 | async-start | bytes 2097152 | tf_op jit(solution)/shard_map/all_to_all | solution.py:60
  236.8 7.7 %copy-start.5 = (f32[1,16,128,128]{3,1,0,2:T(8,128)}, f32[1,16,128,128]{3,1,0,2:T(8,128)S(1)}, u32[]{:S(2)}) copy-start(f32[1,16,128,128]{3,1,0,2:T(8,128)S(1)} %all-to-all-done.1) | copy-start | bytes 3145732
  236.8 29.6 %all-to-all-start = ((f32[1,16,128,128]{3,1,0,2:T(8,128)}), f32[1,16,128,128]{3,1,0,2:T(8,128)S(1)}, u32[]{:S(2)}, u32[]{:S(2)}) async-start(f32[1,16,128,128]{3,1,0,2:T(8,128)} %copy.156), calls=%async_computation.1 | async-start | bytes 2097152 | tf_op jit(solution)/shard_map/all_to_all | solution.py:59
  266.4 1.0 copy-start.7
  267.4 29.8 %all-to-all-start.6 = ((f32[1,128,16,128]{3,2,0,1:T(8,128)}), f32[1,128,16,128]{3,2,0,1:T(8,128)S(1)}, u32[]{:S(2)}, u32[]{:S(2)}) async-start(f32[1,128,16,128]{3,2,0,1:T(8,128)} %copy.194), calls=%async_computation.7 | async-start | bytes 2097152 | tf_op jit(solution)/shard_map/all_to_all | solution.py:75
  272.5 28.9 %copy-start.6 = (f32[1,16,128,128]{3,1,0,2:T(8,128)S(1)}, f32[1,16,128,128]{3,1,0,2:T(8,128)}, u32[]{:S(2)}) copy-start(f32[1,16,128,128]{3,1,0,2:T(8,128)} %copy-done.5) | copy-start | bytes 3145732
  273.8 27.7 %copy-start.8 = (f32[1,16,128,128]{3,1,0,2:T(8,128)S(1)}, f32[1,16,128,128]{3,1,0,2:T(8,128)}, u32[]{:S(2)}) copy-start(f32[1,16,128,128]{3,1,0,2:T(8,128)} %copy-done.7) | copy-start | bytes 3145732
  297.2 29.9 %all-to-all-start.7 = ((f32[1,128,16,128]{3,2,0,1:T(8,128)}), f32[1,128,16,128]{3,2,0,1:T(8,128)}, u32[]{:S(2)}, u32[]{:S(2)}) async-start(f32[1,128,16,128]{3,2,0,1:T(8,128)} %copy.199), calls=%async_computation.8 | async-start | bytes 2097152 | tf_op jit(solution)/shard_map/all_to_all | solution.py:76
  327.1 30.1 %all-to-all-start.3 = ((f32[1,128,16,128]{3,2,0,1:T(8,128)}), f32[1,128,16,128]{3,2,0,1:T(8,128)}, u32[]{:S(2)}, u32[]{:S(2)}) async-start(f32[1,128,16,128]{3,2,0,1:T(8,128)} %copy.173), calls=%async_computation.4 | async-start | bytes 2097152 | tf_op jit(solution)/shard_map/all_to_all | solution.py:76
  357.1 29.7 %all-to-all-start.2 = ((f32[1,128,16,128]{3,2,0,1:T(8,128)}), f32[1,128,16,128]{3,2,0,1:T(8,128)}, u32[]{:S(2)}, u32[]{:S(2)}) async-start(f32[1,128,16,128]{3,2,0,1:T(8,128)} %copy.168), calls=%async_computation.3 | async-start | bytes 2097152 | tf_op jit(solution)/shard_map/all_to_all | solution.py:75
  362.7 4.0 copy-start.4
  394.7 3.7 copy-start.1
Sparse Core Ops, SparseCore 0:
  44.5 41.7 reduce-scatter.1
  88.5 34.4 all-gather.2
where the time goes:
time: 417 us; the launch traced here: 410 us
  waiting for transfers between devices  220 us (53%)
  matrix products  72.7 us (17%)
  starting transfers between devices  34.7 us (8%)
  blocking collectives  28.1 us (7%)
  local copies, waits for them, and re-layouts  23.3 us (6%)
  other arithmetic  16.4 us (4%)
  between operations  14.9 us (4%)
    reduce_scatter x1, waiting for transfers between devices, local(): lax.psum_scatter(jnp.einsum('bk,bxyz->kxyz', own_weights, orbitals, preci...  41.9 us
    all_to_all x2, waiting for transfers between devices, filtered(): lax.all_to_all(imag_part, 'grid', split_axis=2, concat_axis=1, tiled=True)  38.1 us
    all_to_all x2, waiting for transfers between devices, filtered(): lax.all_to_all(back_real, 'grid', split_axis=1, concat_axis=2, tiled=True)  36.9 us
    all_gather x1, waiting for transfers between devices, local(): lax.all_gather(localized, 'band', axis=0, tiled=True)  35.6 us
    all_to_all x2, waiting for transfers between devices, filtered(): lax.all_to_all(real_part, 'grid', split_axis=2, concat_axis=1, tiled=True)  34.3 us
    all_to_all x2, waiting for transfers between devices, filtered(): lax.all_to_all(back_imag, 'grid', split_axis=1, concat_axis=2, tiled=True)  33.2 us
    psum x1, blocking collectives, local(): own_rows = lax.psum(partial_pick, 'grid')  23.1 us
    all_to_all x2, starting transfers between devices, filtered(): lax.all_to_all(real_part, 'grid', split_axis=2, concat_axis=1, tiled=True)  9.43 us
  transfers between devices with their start and end apart: 10, of which 10 were waited for; matrix products, arithmetic and copies ran while one was open for 16% of the time, Pallas kernels for 0%

commit v1 on v0

--- a/solution.py
+++ b/solution.py
@@ -122,7 +122,8 @@
     inside = (local_cell >= 0) & (local_cell < cell_count)
     sampled = jnp.take(flat_local, jnp.clip(local_cell, 0, cell_count - 1), axis=1)
     partial_pick = jnp.where(inside[None, :], sampled, 0.0)
-    own_rows = lax.psum(partial_pick, "grid")
+    parts = lax.all_gather(partial_pick, "grid")
+    own_rows = jnp.sum(parts, axis=0)
     picked = lax.all_gather(own_rows, "band", axis=0, tiled=True)
     gram_matrix = jnp.dot(picked.T, picked, precision=precise)
     factor = jnp.linalg.cholesky(gram_matrix)

time: 417 us -> 422 us (1.012)
    unnamed x0 -> x2, blocking collectives: none -> 28.7 us
    psum x1 -> x0, blocking collectives: 23.1 us -> none  [local(): own_rows = lax.psum(partial_pick, 'grid')]
    all_gather x1 -> x0, blocking collectives: 5.03 us -> none  [local(): picked = lax.all_gather(own_rows, 'band', axis=0, tiled=True)]
  transfers between devices with their start and end apart: 10 -> 10, of which waited for: 10 -> 10; matrix products, arithmetic and copies ran while one was open for 16% -> 15% of each run, Pallas kernels for 0% -> 0%
where the time goes in v1:
time: 422 us; the launch traced here: 415 us
  waiting for transfers between devices  220 us (52%)
  matrix products  72.7 us (17%)
  starting transfers between devices  34.7 us (8%)
  blocking collectives  28.7 us (7%)
  local copies, waits for them, and re-layouts  26.2 us (6%)
  other arithmetic  16.5 us (4%)
  between operations  16.2 us (4%)
    reduce_scatter x1, waiting for transfers between devices, local(): lax.psum_scatter(jnp.einsum('bk,bxyz->kxyz', own_weights, orbitals, preci...  42.1 us
    all_to_all x2, waiting for transfers between devices, filtered(): lax.all_to_all(imag_part, 'grid', split_axis=2, concat_axis=1, tiled=True)  38.1 us
    all_to_all x2, waiting for transfers between devices, filtered(): lax.all_to_all(back_real, 'grid', split_axis=1, concat_axis=2, tiled=True)  36.9 us
    all_gather x1, waiting for transfers between devices, local(): lax.all_gather(localized, 'band', axis=0, tiled=True)  35.6 us
    all_to_all x2, waiting for transfers between devices, filtered(): lax.all_to_all(real_part, 'grid', split_axis=2, concat_axis=1, tiled=True)  34.3 us
    all_to_all x2, waiting for transfers between devices, filtered(): lax.all_to_all(back_imag, 'grid', split_axis=1, concat_axis=2, tiled=True)  33.1 us
    unnamed x2, blocking collectives  28.7 us
    all_to_all x2, starting transfers between devices, filtered(): lax.all_to_all(real_part, 'grid', split_axis=2, concat_axis=1, tiled=True)  9.43 us
  transfers between devices with their start and end apart: 10, of which 10 were waited for; matrix products, arithmetic and copies ran while one was open for 15% of the time, Pallas kernels for 0%

profile of v1, /device:TPU:0, one launch (start us, length us, event | category | flops | bytes accessed | tf_op | source)
XLA Modules:
  0.0 415.2 jit_solution(1817917066573318548)
XLA Ops:
  13.8 23.1 %all-reduce = f32[32]{0:T(128)S(1)} all-reduce(f32[32]{0:T(128)S(1)} %fusion.158), channel_id=2, replica_groups=mesh['band'=4,'grid'=8] {'grid'}, use_global_device_ids=true, to_apply=%add | all-reduce | flops 32 | bytes 256
  37.3 5.6 %all-reduce.1 = f32[16]{0:T(128)S(1)} all-reduce(f32[16]{0:T(128)S(1)} %dynamic-update-slice.4), channel_id=3, replica_groups=mesh['band'=4,'grid'=8] {'band'}, use_global_device_ids=true, to_apply=%add.1 | all-reduce | flops 16 | bytes 128
  45.5 3.7 broadcast_multiply_fusion
  49.3 42.1 %reduce-scatter.2.cloned.1.call-done = f32[1,16,128,128]{3,2,1,0:T(8,128)} async-done(((f32[4,16,128,128]{3,2,1,0:T(8,128)}), f32[1,16,128,128]{3,2,1,0:T(8,128)}) %reduce-scatter.2.cloned.1.call-update) | async-done | bytes 1048592 | tf_op jit(solution)/shard_map/reduce_scatter | solution.py:132
  92.6 35.6 %all-gather.4.cloned.1.call-done = f32[4,16,128,128]{3,2,1,0:T(8,128)} async-done(((f32[1,16,128,128]{3,2,1,0:T(8,128)}), f32[4,16,128,128]{3,2,1,0:T(8,128)}) %all-gather.4.cloned.1.call-update) | async-done | bytes 4194320 | tf_op jit(solution)/shard_map/all_gather | solution.py:152
  128.2 8.5 %fusion = f32[4,16,128,128]{3,0,2,1:T(4,128)S(1)} fusion(f32[4,16,128,128]{3,2,1,0:T(8,128)} %all-gather.4.cloned.1.call-done, s32[4]{0:T(128)S(1)} %broadcast_select_fusion), kind=kOutput, calls=%fused_computation.1 | convolution fusion | flops 50331664 | bytes 8388624 | tf_op jit(solution)/shard_map/qm,mxyz->qxyz/dot_general | solution.py:109
  136.7 3.6 slice_multiply_fusion.3
  148.8 1.6 copy.182
  150.4 5.8 %all-to-all-start.4 = ((f32[1,16,128,128]{3,1,0,2:T(8,128)}), f32[1,16,128,128]{3,1,0,2:T(8,128)}, u32[]{:S(2)}, u32[]{:S(2)}) async-start(f32[1,16,128,128]{3,1,0,2:T(8,128)} %copy.182), calls=%async_computation.5 | async-start | bytes 2097152 | tf_op jit(solution)/shard_map/all_to_all | solution.py:59
  157.4 2.5 fusion.8
  161.5 20.8 %all-to-all-done.4 = f32[1,16,128,128]{3,1,0,2:T(8,128)} async-done(((f32[1,16,128,128]{3,1,0,2:T(8,128)}), f32[1,16,128,128]{3,1,0,2:T(8,128)}, u32[]{:S(2)}, u32[]{:S(2)}) %all-to-all-start.4) | async-done | bytes 1048608 | tf_op jit(solution)/shard_map/all_to_all | solution.py:59
  182.4 4.3 %all-to-all-start.5 = ((f32[1,16,128,128]{3,1,0,2:T(8,128)}), f32[1,16,128,128]{3,1,0,2:T(8,128)}, u32[]{:S(2)}, u32[]{:S(2)}) async-start(f32[1,16,128,128]{3,1,0,2:T(8,128)} %copy.187), calls=%async_computation.6 | async-start | bytes 2097152 | tf_op jit(solution)/shard_map/all_to_all | solution.py:60
  194.1 1.6 copy.161
  195.7 16.5 %all-to-all-done.5 = f32[1,16,128,128]{3,1,0,2:T(8,128)} async-done(((f32[1,16,128,128]{3,1,0,2:T(8,128)}), f32[1,16,128,128]{3,1,0,2:T(8,128)}, u32[]{:S(2)}, u32[]{:S(2)}) %all-to-all-start.5) | async-done | bytes 1048608 | tf_op jit(solution)/shard_map/all_to_all | solution.py:60
  212.2 4.0 all-to-all-start.1
  218.8 1.6 copy.156
  220.4 21.6 %all-to-all-done.1 = f32[1,16,128,128]{3,1,0,2:T(8,128)S(1)} async-done(((f32[1,16,128,128]{3,1,0,2:T(8,128)}), f32[1,16,128,128]{3,1,0,2:T(8,128)S(1)}, u32[]{:S(2)}, u32[]{:S(2)}) %all-to-all-start.1) | async-done | bytes 1048608 | tf_op jit(solution)/shard_map/all_to_all | solution.py:60
  242.0 3.6 all-to-all-start
  256.5 1.6 copy.194
  258.1 13.5 %all-to-all-done = f32[1,16,128,128]{3,1,0,2:T(8,128)S(1)} async-done(((f32[1,16,128,128]{3,1,0,2:T(8,128)}), f32[1,16,128,128]{3,1,0,2:T(8,128)S(1)}, u32[]{:S(2)}, u32[]{:S(2)}) %all-to-all-start) | async-done | bytes 1048608 | tf_op jit(solution)/shard_map/all_to_all | solution.py:59
  272.6 3.8 all-to-all-start.6
  280.6 21.8 %all-to-all-done.6 = f32[1,128,16,128]{3,2,0,1:T(8,128)S(1)} async-done(((f32[1,128,16,128]{3,2,0,1:T(8,128)}), f32[1,128,16,128]{3,2,0,1:T(8,128)S(1)}, u32[]{:S(2)}, u32[]{:S(2)}) %all-to-all-start.6) | async-done | bytes 1048608 | tf_op jit(solution)/shard_map/all_to_all | solution.py:75
  302.3 4.2 %all-to-all-start.7 = ((f32[1,128,16,128]{3,2,0,1:T(8,128)}), f32[1,128,16,128]{3,2,0,1:T(8,128)}, u32[]{:S(2)}, u32[]{:S(2)}) async-start(f32[1,128,16,128]{3,2,0,1:T(8,128)} %copy.199), calls=%async_computation.8 | async-start | bytes 2097152 | tf_op jit(solution)/shard_map/all_to_all | solution.py:76
  315.0 1.6 copy.173
  316.6 15.6 %all-to-all-done.7 = f32[1,128,16,128]{3,2,0,1:T(8,128)} async-done(((f32[1,128,16,128]{3,2,0,1:T(8,128)}), f32[1,128,16,128]{3,2,0,1:T(8,128)}, u32[]{:S(2)}, u32[]{:S(2)}) %all-to-all-start.7) | async-done | bytes 1048608 | tf_op jit(solution)/shard_map/all_to_all | solution.py:76
  332.2 4.6 %all-to-all-start.3 = ((f32[1,128,16,128]{3,2,0,1:T(8,128)}), f32[1,128,16,128]{3,2,0,1:T(8,128)}, u32[]{:S(2)}, u32[]{:S(2)}) async-start(f32[1,128,16,128]{3,2,0,1:T(8,128)} %copy.173), calls=%async_computation.4 | async-start | bytes 2097152 | tf_op jit(solution)/shard_map/all_to_all | solution.py:76
  339.5 1.6 copy.168
  342.5 2.3 fusion.48
  344.8 17.5 %all-to-all-done.3 = f32[1,128,16,128]{3,2,0,1:T(8,128)} async-done(((f32[1,128,16,128]{3,2,0,1:T(8,128)}), f32[1,128,16,128]{3,2,0,1:T(8,128)}, u32[]{:S(2)}, u32[]{:S(2)}) %all-to-all-start.3) | async-done | bytes 1048608 | tf_op jit(solution)/shard_map/all_to_all | solution.py:76
  362.3 4.2 %all-to-all-start.2 = ((f32[1,128,16,128]{3,2,0,1:T(8,128)}), f32[1,128,16,128]{3,2,0,1:T(8,128)}, u32[]{:S(2)}, u32[]{:S(2)}) async-start(f32[1,128,16,128]{3,2,0,1:T(8,128)} %copy.168), calls=%async_computation.3 | async-start | bytes 2097152 | tf_op jit(solution)/shard_map/all_to_all | solution.py:75
  376.8 15.1 %all-to-all-done.2 = f32[1,128,16,128]{3,2,0,1:T(8,128)} async-done(((f32[1,128,16,128]{3,2,0,1:T(8,128)}), f32[1,128,16,128]{3,2,0,1:T(8,128)}, u32[]{:S(2)}, u32[]{:S(2)}) %all-to-all-start.2) | async-done | bytes 1048608 | tf_op jit(solution)/shard_map/all_to_all | solution.py:75
  403.6 4.5 %multiply_add_fusion = f32[1,16,128,128]{3,0,2,1:T(1,128)} fusion(f32[1,16,128,128]{3,0,2,1:T(1,128)S(1)} %bitcast.316, f32[1,16,128,128]{3,0,2,1:T(1,128)S(1)} %bitcast.315, f32[1,16,128,128]{3,0,2,1:T(1,128)S(1)} %bitcast.317, f32[1,16,128,128]{3,0,2,1:T(1,128)S(1)} %bitcast.318, f32[4,16,128,128]{3,0,2,1:T(4,128)S(1)} %copy-done.1), kind=kLoop, calls=%fused_computation.49 | loop fusion | flops 1835008 | bytes 9437184 | tf_op jit(solution)/shard_map/add | solution.py:160
  (109 shorter events, 80.8 us)
Async XLA Ops:
  7.2 84.3 %reduce-scatter.2.cloned.1.call-start = ((), (), s32[]{:S(2)}) async-start(), calls=%async_computation.9 | async-start | bytes 5242880 | tf_op jit(solution)/shard_map/reduce_scatter | solution.py:132
  49.3 78.9 %all-gather.4.cloned.1.call-start = ((), (), s32[]{:S(2)}) async-start(), calls=%async_computation.10 | async-start | bytes 5242880 | tf_op jit(solution)/shard_map/all_gather | solution.py:152
  92.6 44.1 %copy-start.3 = (f32[1,16,128,128]{3,2,1,0:T(8,128)S(1)}, f32[1,16,128,128]{3,2,1,0:T(8,128)}, u32[]{:S(2)}) copy-start(f32[1,16,128,128]{3,2,1,0:T(8,128)} %reduce-scatter.2.cloned.1.call-done) | copy-start | bytes 3145732
  136.7 3.6 copy-start
  145.2 1.0 copy-start.2
  150.4 32.0 %all-to-all-start.4 = ((f32[1,16,128,128]{3,1,0,2:T(8,128)}), f32[1,16,128,128]{3,1,0,2:T(8,128)}, u32[]{:S(2)}, u32[]{:S(2)}) async-start(f32[1,16,128,128]{3,1,0,2:T(8,128)} %copy.182), calls=%async_computation.5 | async-start | bytes 2097152 | tf_op jit(solution)/shard_map/all_to_all | solution.py:59
  182.4 29.9 %all-to-all-start.5 = ((f32[1,16,128,128]{3,1,0,2:T(8,128)}), f32[1,16,128,128]{3,1,0,2:T(8,128)}, u32[]{:S(2)}, u32[]{:S(2)}) async-start(f32[1,16,128,128]{3,1,0,2:T(8,128)} %copy.187), calls=%async_computation.6 | async-start | bytes 2097152 | tf_op jit(solution)/shard_map/all_to_all | solution.py:60
  212.2 29.7 %all-to-all-start.1 = ((f32[1,16,128,128]{3,1,0,2:T(8,128)}), f32[1,16,128,128]{3,1,0,2:T(8,128)S(1)}, u32[]{:S(2)}, u32[]{:S(2)}) async-start(f32[1,16,128,128]{3,1,0,2:T(8,128)} %copy.161), calls=%async_computation.2 | async-start | bytes 2097152 | tf_op jit(solution)/shard_map/all_to_all | solution.py:60
  242.0 7.7 %copy-start.5 = (f32[1,16,128,128]{3,1,0,2:T(8,128)}, f32[1,16,128,128]{3,1,0,2:T(8,128)S(1)}, u32[]{:S(2)}) copy-start(f32[1,16,128,128]{3,1,0,2:T(8,128)S(1)} %all-to-all-done.1) | copy-start | bytes 3145732
  242.0 29.6 %all-to-all-start = ((f32[1,16,128,128]{3,1,0,2:T(8,128)}), f32[1,16,128,128]{3,1,0,2:T(8,128)S(1)}, u32[]{:S(2)}, u32[]{:S(2)}) async-start(f32[1,16,128,128]{3,1,0,2:T(8,128)} %copy.156), calls=%async_computation.1 | async-start | bytes 2097152 | tf_op jit(solution)/shard_map/all_to_all | solution.py:59
  271.6 1.0 copy-start.7
  272.6 29.8 %all-to-all-start.6 = ((f32[1,128,16,128]{3,2,0,1:T(8,128)}), f32[1,128,16,128]{3,2,0,1:T(8,128)S(1)}, u32[]{:S(2)}, u32[]{:S(2)}) async-start(f32[1,128,16,128]{3,2,0,1:T(8,128)} %copy.194), calls=%async_computation.7 | async-start | bytes 2097152 | tf_op jit(solution)/shard_map/all_to_all | solution.py:75
  277.7 28.9 %copy-start.6 = (f32[1,16,128,128]{3,1,0,2:T(8,128)S(1)}, f32[1,16,128,128]{3,1,0,2:T(8,128)}, u32[]{:S(2)}) copy-start(f32[1,16,128,128]{3,1,0,2:T(8,128)} %copy-done.5) | copy-start | bytes 3145732
  279.0 27.7 %copy-start.8 = (f32[1,16,128,128]{3,1,0,2:T(8,128)S(1)}, f32[1,16,128,128]{3,1,0,2:T(8,128)}, u32[]{:S(2)}) copy-start(f32[1,16,128,128]{3,1,0,2:T(8,128)} %copy-done.7) | copy-start | bytes 3145732
  302.3 29.9 %all-to-all-start.7 = ((f32[1,128,16,128]{3,2,0,1:T(8,128)}), f32[1,128,16,128]{3,2,0,1:T(8,128)}, u32[]{:S(2)}, u32[]{:S(2)}) async-start(f32[1,128,16,128]{3,2,0,1:T(8,128)} %copy.199), calls=%async_computation.8 | async-start | bytes 2097152 | tf_op jit(solution)/shard_map/all_to_all | solution.py:76
  332.2 30.1 %all-to-all-start.3 = ((f32[1,128,16,128]{3,2,0,1:T(8,128)}), f32[1,128,16,128]{3,2,0,1:T(8,128)}, u32[]{:S(2)}, u32[]{:S(2)}) async-start(f32[1,128,16,128]{3,2,0,1:T(8,128)} %copy.173), calls=%async_computation.4 | async-start | bytes 2097152 | tf_op jit(solution)/shard_map/all_to_all | solution.py:76
  362.3 29.7 %all-to-all-start.2 = ((f32[1,128,16,128]{3,2,0,1:T(8,128)}), f32[1,128,16,128]{3,2,0,1:T(8,128)}, u32[]{:S(2)}, u32[]{:S(2)}) async-start(f32[1,128,16,128]{3,2,0,1:T(8,128)} %copy.168), calls=%async_computation.3 | async-start | bytes 2097152 | tf_op jit(solution)/shard_map/all_to_all | solution.py:75
  367.9 4.0 copy-start.4
  399.9 3.7 copy-start.1
Sparse Core Ops, SparseCore 0:
  49.4 41.9 reduce-scatter.1
  93.6 34.4 all-gather.3
